TPU v7x, 32 devices: a whole 2x2x4 slice. The times are simulated.
32 devices in a mesh: pts: 4 (over x, core), snap: 8 (over z, y).
Axes of the slice: x: 2, y: 2, z: 4, core: 2. Of those that a mesh axis runs over, the one named last changes fastest.
Arguments:
- snapshots: float32 [4096, 8192], P('pts', 'snap'), may hold values from -8 to 8
- modes_init: float32 [4096, 128], P('pts'), may hold values from -6 to 6
- coefs_init: float32 [128, 8192], P(None, 'snap'), may hold values from -0.09375 to 0.09375
Outputs:
- modes: float32 [4096, 128], P('pts')
- amplitudes: float32 [128, 8192], P(None, 'snap')
All inputs are finite; a program needn't handle non-finite values.
Results may differ from a plain program's by a relative error of at most 0.0003.
Values sent between devices are 32-bit elements; how exact they have to be, the bound alone decides.
A program may use at most 64 MiB of HBM per device.

v0:
```python
import jax
import jax.numpy as jnp
from jax import lax
from jax.sharding import PartitionSpec as P

OUTER = 2
INNER = 2
HUBER = 1.345
RIDGE = 0.01


def high_dot(left, right):
    return jnp.dot(left, right, preferred_element_type=jnp.float32, precision=lax.Precision.HIGHEST)


def clipped_error(snapshots, modes, coefs, count):
    error = snapshots - high_dot(modes, coefs)
    total = lax.psum(jnp.sum(error * error), ("pts", "snap"))
    limit = HUBER * jnp.sqrt(total / count + 1e-06)
    return jnp.clip(error, -limit, limit)


def shards(snapshots, modes_init, coefs_init):
    modes = modes_init
    coefs = coefs_init
    rows, width = snapshots.shape
    points = rows * lax.axis_size("pts")
    count = float(points * width * lax.axis_size("snap"))
    rank = modes.shape[1]
    eye = jnp.eye(rank, dtype=jnp.float32)
    for outer in range(OUTER):
        gram = lax.psum(high_dot(modes.T, modes), "pts") + RIDGE * eye
        factor = jnp.linalg.cholesky(gram)
        for inner in range(INNER):
            clipped = clipped_error(snapshots, modes, coefs, count)
            product = high_dot(modes.T, clipped)
            share = lax.psum_scatter(product, "pts", scatter_dimension=1, tiled=True)
            span = share.shape[1]
            own = lax.dynamic_slice_in_dim(coefs, lax.axis_index("pts") * span, span, 1)
            own = own + jax.scipy.linalg.cho_solve((factor, True), share)
            coefs = lax.all_gather(own, "pts", axis=1, tiled=True)
        clipped = clipped_error(snapshots, modes, coefs, count)
        hess = lax.psum(high_dot(coefs, coefs.T), "snap") + RIDGE * eye
        hfactor = jnp.linalg.cholesky(hess)
        moment = high_dot(clipped, coefs.T)
        summed = lax.psum(moment, "snap")
        modes = modes + jax.scipy.linalg.cho_solve((hfactor, True), summed.T).T
    return (modes, coefs * jnp.sqrt(jnp.float32(points)))


def solution(mesh):
    in_specs = (P("pts", "snap"), P("pts", None), P(None, "snap"))
    out_specs = (P("pts", None), P(None, "snap"))
    return jax.shard_map(shards, mesh=mesh, in_specs=in_specs, out_specs=out_specs, check_vma=False)
```

profile of v0, /device:TPU:0, one launch (start us, length us, event | category | flops | bytes accessed | tf_op | source)
XLA Modules:
  0.0 692.1 jit_solution(7492501816023668363)
XLA Ops:
  10.1 8.6 %multiply_reduce_fusion.5 = (f32[]{:T(128)}, f32[1024,1024]{1,0:T(8,128)}) fusion(f32[1024,1024]{1,0:T(8,128)} %param.8, f32[1024,128]{1,0:T(8,128)} %param.9, f32[128,1024]{1,0:T(8,128)} %param.10), kind=kOutput, calls=%fused_computation.25 | convolution fusion | flops 1613758464 | bytes 9437188 | tf_op jit(solution)/shard_map/dot_general | solution.py:13
  18.8 42.5 %psum.85 = f32[]{:T(128)} all-reduce(f32[]{:T(128)} %get-tuple-element.11), channel_id=1, replica_groups=mesh['pts'=4,'snap'=8] {'pts','snap'}, use_global_device_ids=true, to_apply=%region_4.6 | all-reduce | flops 1 | bytes 8 | tf_op jit(solution)/shard_map/psum | solution.py:18
  61.9 9.6 %fusion.32 = f32[128,1024]{0,1:T(8,128)} fusion(f32[1024,128]{1,0:T(8,128)S(1)} %copy-done, f32[1024,1024]{1,0:T(8,128)} %get-tuple-element.12, f32[]{:T(128)S(6)} %neg.18, f32[]{:T(128)S(6)} %mul.63), kind=kOutput, calls=%fused_computation.46 | convolution fusion | flops 1612709888 | bytes 5242888 | tf_op jit(solution)/shard_map/dot_general | solution.py:13
  79.4 11.7 %cholesky.74 = f32[128,128]{1,0:T(8,128)S(1)} custom-call(f32[128,128]{1,0:T(8,128)S(1)} %fusion.63), custom_call_target="Cholesky" | custom-call | tf_op jit(solution)/shard_map/jit(cholesky)/cholesky | solution.py:33
  92.4 9.8 %custom-call.16 = f32[1,128,128]{1,2,0:T(8,128)S(1)} custom-call(f32[1,128,128]{2,1,0:T(8,128)S(1)} %fusion.38), custom_call_target="InvertDiagBlocksLowerTriangular" | custom-call | tf_op jit(solution)/shard_map/jit(_cho_solve)/triangular_solve | solution.py:40
  104.7 8.0 %all_gather.12 = f32[128,1024]{1,0:T(8,128)S(1)} all-gather(f32[128,256]{1,0:T(8,128)S(1)} %convolution_add_fusion.3), channel_id=1, replica_groups=mesh['pts'=4,'snap'=8] {'pts'}, dimensions={1}, use_global_device_ids=true | all-gather | bytes 655360 | tf_op jit(solution)/shard_map/all_gather | solution.py:41
  112.6 7.7 %multiply_reduce_fusion.4 = (f32[]{:T(128)}, f32[1024,1024]{0,1:T(8,128)}) fusion(f32[1024,1024]{0,1:T(8,128)} %copy.7, f32[128,1024]{1,0:T(8,128)S(1)} %all_gather.12, f32[1024,128]{1,0:T(8,128)S(1)} %copy-done), kind=kOutput, calls=%fused_computation.21 | convolution fusion | flops 1613758464 | bytes 9437188 | tf_op jit(solution)/shard_map/dot_general | solution.py:13
  120.3 39.7 %psum.86 = f32[]{:T(128)} all-reduce(f32[]{:T(128)} %get-tuple-element.13), channel_id=1, replica_groups=mesh['pts'=4,'snap'=8] {'pts','snap'}, use_global_device_ids=true, to_apply=%region_7.10 | all-reduce | flops 1 | bytes 8 | tf_op jit(solution)/shard_map/psum | solution.py:18
  160.7 6.4 fusion.35
  167.2 22.0 %reduce-scatter.7.cloned.1.call-done = f32[128,256]{0,1:T(8,128)} async-done(((f32[128,1024]{0,1:T(8,128)}), f32[128,256]{0,1:T(8,128)}) %reduce-scatter.7.cloned.1.call-update) | async-done | bytes 131088 | tf_op jit(solution)/shard_map/reduce_scatter | solution.py:37
  190.7 6.6 all_gather.13
  197.3 7.6 %multiply_reduce_fusion.3 = (f32[]{:T(128)}, f32[1024,1024]{0,1:T(8,128)}) fusion(f32[1024,1024]{0,1:T(8,128)} %copy.7, f32[128,1024]{1,0:T(8,128)S(1)} %all_gather.13, f32[1024,128]{1,0:T(8,128)S(1)} %copy-done), kind=kOutput, calls=%fused_computation.17 | convolution fusion | flops 1613758464 | bytes 9437188 | tf_op jit(solution)/shard_map/dot_general | solution.py:13
  206.1 40.0 %psum.88 = f32[]{:T(128)} all-reduce(f32[]{:T(128)} %get-tuple-element.15), channel_id=1, replica_groups=mesh['pts'=4,'snap'=8] {'pts','snap'}, use_global_device_ids=true, to_apply=%region_11.14 | all-reduce | flops 1 | bytes 8 | tf_op jit(solution)/shard_map/psum | solution.py:18
  246.8 5.7 fusion.9
  253.0 73.4 %all-reduce.13.cloned.1.call-done = (f32[128,1024]{1,0:T(8,128)}, f32[128,128]{0,1:T(8,128)}) async-done(((f32[128,1024]{1,0:T(8,128)}, f32[128,128]{0,1:T(8,128)}), (f32[128,1024]{1,0:T(8,128)}, f32[128,128]{0,1:T(8,128)})) %all-reduce.13.cloned.1.call-update) | async-done | bytes 589840 | tf_op jit(solution)/shard_map/psum | solution.py:46
  328.2 11.7 %cholesky.85 = f32[128,128]{1,0:T(8,128)S(1)} custom-call(f32[128,128]{1,0:T(8,128)S(1)} %fusion.56), custom_call_target="Cholesky" | custom-call | tf_op jit(solution)/shard_map/jit(cholesky)/cholesky | solution.py:44
  341.3 9.8 %custom-call.18 = f32[1,128,128]{1,2,0:T(8,128)S(1)} custom-call(f32[1,128,128]{2,1,0:T(8,128)S(1)} %fusion.39), custom_call_target="InvertDiagBlocksLowerTriangular" | custom-call | tf_op jit(solution)/shard_map/jit(_cho_solve)/triangular_solve | solution.py:47
  354.6 7.6 %multiply_reduce_fusion.2 = (f32[]{:T(128)}, f32[1024,1024]{1,0:T(8,128)}) fusion(f32[1024,1024]{1,0:T(8,128)} %param.8, f32[1024,128]{0,1:T(8,128)S(1)} %fusion.30, f32[128,1024]{1,0:T(8,128)S(1)} %all_gather.13), kind=kOutput, calls=%fused_computation.13 | convolution fusion | flops 1613758464 | bytes 9437188 | tf_op jit(solution)/shard_map/dot_general | solution.py:13
  362.2 40.0 %psum.91 = f32[]{:T(128)} all-reduce(f32[]{:T(128)} %get-tuple-element.17), channel_id=1, replica_groups=mesh['pts'=4,'snap'=8] {'pts','snap'}, use_global_device_ids=true, to_apply=%region_15.19 | all-reduce | flops 1 | bytes 8 | tf_op jit(solution)/shard_map/psum | solution.py:18
  410.5 11.7 %cholesky.96 = f32[128,128]{1,0:T(8,128)S(1)} custom-call(f32[128,128]{1,0:T(8,128)S(1)} %fusion.52), custom_call_target="Cholesky" | custom-call | tf_op jit(solution)/shard_map/jit(cholesky)/cholesky | solution.py:33
  423.6 9.8 %custom-call.19 = f32[1,128,128]{1,2,0:T(8,128)S(1)} custom-call(f32[1,128,128]{2,1,0:T(8,128)S(1)} %fusion.40), custom_call_target="InvertDiagBlocksLowerTriangular" | custom-call | tf_op jit(solution)/shard_map/jit(_cho_solve)/triangular_solve | solution.py:40
  434.9 8.1 %all_gather.14 = f32[128,1024]{1,0:T(8,128)S(1)} all-gather(f32[128,256]{1,0:T(8,128)S(1)} %convolution_add_fusion.1), channel_id=1, replica_groups=mesh['pts'=4,'snap'=8] {'pts'}, dimensions={1}, use_global_device_ids=true | all-gather | bytes 655360 | tf_op jit(solution)/shard_map/all_gather | solution.py:41
  443.1 7.6 %multiply_reduce_fusion.1 = (f32[]{:T(128)}, f32[1024,1024]{1,0:T(8,128)}) fusion(f32[1024,1024]{1,0:T(8,128)} %param.8, f32[1024,128]{0,1:T(8,128)S(1)} %fusion.30, f32[128,1024]{1,0:T(8,128)S(1)} %all_gather.14), kind=kOutput, calls=%fused_computation.9 | convolution fusion | flops 1613758464 | bytes 9437188 | tf_op jit(solution)/shard_map/dot_general | solution.py:13
  450.6 38.7 %psum.92 = f32[]{:T(128)} all-reduce(f32[]{:T(128)} %get-tuple-element.19), channel_id=1, replica_groups=mesh['pts'=4,'snap'=8] {'pts','snap'}, use_global_device_ids=true, to_apply=%region_18.22 | all-reduce | flops 1 | bytes 8 | tf_op jit(solution)/shard_map/psum | solution.py:18
  495.8 22.3 %reduce-scatter.11.cloned.1.call-done = f32[128,256]{1,0:T(8,128)} async-done(((f32[128,1024]{1,0:T(8,128)}), f32[128,256]{1,0:T(8,128)}) %reduce-scatter.11.cloned.1.call-update) | async-done | bytes 131088 | tf_op jit(solution)/shard_map/reduce_scatter | solution.py:37
  519.6 6.6 all_gather.15
  526.2 7.6 %multiply_reduce_fusion = (f32[]{:T(128)}, f32[1024,1024]{1,0:T(8,128)}) fusion(f32[1024,1024]{1,0:T(8,128)} %param.8, f32[1024,128]{0,1:T(8,128)S(1)} %fusion.30, f32[128,1024]{1,0:T(8,128)S(1)} %all_gather.15), kind=kOutput, calls=%fused_computation.5 | convolution fusion | flops 1613758464 | bytes 9437188 | tf_op jit(solution)/shard_map/dot_general | solution.py:13
  535.0 40.2 %psum.94 = f32[]{:T(128)} all-reduce(f32[]{:T(128)} %get-tuple-element.21), channel_id=1, replica_groups=mesh['pts'=4,'snap'=8] {'pts','snap'}, use_global_device_ids=true, to_apply=%region_22.26 | all-reduce | flops 1 | bytes 8 | tf_op jit(solution)/shard_map/psum | solution.py:18
  575.9 7.3 %fusion = f32[128,1024]{1,0:T(8,128)} fusion(f32[128,1024]{1,0:T(8,128)S(1)} %all_gather.15, f32[1024,1024]{1,0:T(8,128)} %get-tuple-element.22, f32[]{:T(128)S(6)} %neg.23, f32[]{:T(128)S(6)} %mul.73), kind=kOutput, calls=%fused_computation.2 | convolution fusion | flops 1612709888 | bytes 5242888 | tf_op jit(solution)/shard_map/dot_general | solution.py:13
  584.1 73.0 %all-reduce.11.cloned.1.call-done = (f32[128,1024]{1,0:T(8,128)}, f32[128,128]{0,1:T(8,128)}) async-done(((f32[128,1024]{1,0:T(8,128)}, f32[128,128]{0,1:T(8,128)}), (f32[128,1024]{1,0:T(8,128)}, f32[128,128]{0,1:T(8,128)})) %all-reduce.11.cloned.1.call-update) | async-done | bytes 589840 | tf_op jit(solution)/shard_map/psum | solution.py:46
  658.9 11.7 %cholesky.107 = f32[128,128]{1,0:T(8,128)S(1)} custom-call(f32[128,128]{1,0:T(8,128)S(1)} %fusion.45), custom_call_target="Cholesky" | custom-call | tf_op jit(solution)/shard_map/jit(cholesky)/cholesky | solution.py:44
  672.0 9.8 %custom-call.21 = f32[1,128,128]{1,2,0:T(8,128)S(1)} custom-call(f32[1,128,128]{2,1,0:T(8,128)S(1)} %fusion.41), custom_call_target="InvertDiagBlocksLowerTriangular" | custom-call | tf_op jit(solution)/shard_map/jit(_cho_solve)/triangular_solve | solution.py:47
  (68 shorter events, 50.3 us)
Async XLA Ops:
  7.2 70.4 %all-reduce.7.cloned.1.call-start = ((), (), s32[]{:S(2)}) async-start(), calls=%async_computation.4 | async-start | bytes 131072 | tf_op jit(solution)/shard_map/psum | solution.py:32
  10.1 51.9 %copy-start = (f32[1024,128]{1,0:T(8,128)S(1)}, f32[1024,128]{1,0:T(8,128)}, u32[]{:S(2)}) copy-start(f32[1024,128]{1,0:T(8,128)} %param.9) | copy-start | bytes 1572868
  10.1 92.2 %reduce-scatter.5.cloned.1.call-start = ((), (), s32[]{:S(2)}) async-start(), calls=%async_computation.5 | async-start | bytes 655360 | tf_op jit(solution)/shard_map/reduce_scatter | solution.py:37
  71.6 117.6 %reduce-scatter.7.cloned.1.call-start = ((), (), s32[]{:S(2)}) async-start(), calls=%async_computation.6 | async-start | bytes 655360 | tf_op jit(solution)/shard_map/reduce_scatter | solution.py:37
  167.1 159.3 %all-reduce.13.cloned.1.call-start = ((), (), s32[]{:S(2)}) async-start(), calls=%async_computation.11 | async-start | bytes 1179648 | tf_op jit(solution)/shard_map/psum | solution.py:46
  252.5 156.2 %all-reduce.9.cloned.1.call-start = ((), (), s32[]{:S(2)}) async-start(), calls=%async_computation.7 | async-start | bytes 131072 | tf_op jit(solution)/shard_map/psum | solution.py:32
  362.2 71.2 %reduce-scatter.9.cloned.1.call-start = ((), (), s32[]{:S(2)}) async-start(), calls=%async_computation.8 | async-start | bytes 655360 | tf_op jit(solution)/shard_map/reduce_scatter | solution.py:37
  408.6 109.5 %reduce-scatter.11.cloned.1.call-start = ((), (), s32[]{:S(2)}) async-start(), calls=%async_computation.9 | async-start | bytes 655360 | tf_op jit(solution)/shard_map/reduce_scatter | solution.py:37
  495.8 161.4 %all-reduce.11.cloned.1.call-start = ((), (), s32[]{:S(2)}) async-start(), calls=%async_computation.10 | async-start | bytes 1179648 | tf_op jit(solution)/shard_map/psum | solution.py:46
Sparse Core Ops, SparseCore 0:
  10.9 34.2 all-reduce.6
  71.7 21.8 reduce-scatter.4
  167.3 21.8 reduce-scatter.6
  252.7 73.7 all-reduce.12
  362.3 30.6 all-reduce.8
  408.8 21.6 reduce-scatter.8
  495.9 22.2 reduce-scatter.10
  583.4 73.6 all-reduce.10
where the time goes:
time: 698 us; the launch traced here: 692 us
  blocking collectives  270 us (39%)
  waiting for transfers between devices  191 us (27%)
  matrix products  105 us (15%)
  other arithmetic  99.1 us (14%)
  between operations  18.8 us (3%)
    psum x6, blocking collectives, clipped_error(): total = lax.psum(jnp.sum(error * error), ('pts', 'snap'))  241 us
    psum x2, waiting for transfers between devices, shards(): summed = lax.psum(moment, 'snap')  146 us
    dot_general x16, matrix products, high_dot(): jnp.dot(left, right, preferred_element_type=jnp.float32, precision=lax.Pr...  93.5 us
    reduce_scatter x4, waiting for transfers between devices, shards(): share = lax.psum_scatter(product, 'pts', scatter_dimension=1, tiled=True)  44.4 us
    all_gather x4, blocking collectives, shards(): coefs = lax.all_gather(own, 'pts', axis=1, tiled=True)  29.3 us
    another operation x6, other arithmetic, shards(): factor = jnp.linalg.cholesky(gram)  24.8 us
    another operation x6, other arithmetic, shards(): hfactor = jnp.linalg.cholesky(hess)  24.8 us
    another operation x4, other arithmetic, shards(): own = own + jax.scipy.linalg.cho_solve((factor, True), share)  20.9 us
  transfers between devices with their start and end apart: 8, of which 4 were waited for; matrix products, arithmetic and copies ran while one was open for 12% of the time, Pallas kernels for 0%

commit v1 on v0

--- a/solution.py
+++ b/solution.py
@@ -43,7 +43,11 @@
         hess = lax.psum(high_dot(coefs, coefs.T), "snap") + RIDGE * eye
         hfactor = jnp.linalg.cholesky(hess)
         moment = high_dot(clipped, coefs.T)
-        summed = lax.psum(moment, "snap")
+        count_2 = lax.axis_size("snap")
+        summed, far = (moment, 1)
+        while far < count_2:
+            summed = summed + lax.ppermute(summed, "snap", [(i, i ^ far) for i in range(count_2)])
+            far = 2 * far
         modes = modes + jax.scipy.linalg.cho_solve((hfactor, True), summed.T).T
     return (modes, coefs * jnp.sqrt(jnp.float32(points)))
 

time: 698 us -> 720 us (1.032)
  starting transfers between devices: 1.07 us -> 12.8 us
  waiting for transfers between devices: 191 us -> 202 us
    ppermute x0 -> x6, waiting for transfers between devices: none -> 21.2 us  [shards(): lax.ppermute(summed, 'snap', [(i, i ^ far) for i in range(count_2)])]
    ppermute x0 -> x6, starting transfers between devices: none -> 11.8 us  [shards(): lax.ppermute(summed, 'snap', [(i, i ^ far) for i in range(count_2)])]
    psum x2, waiting for transfers between devices: 146 us -> 137 us  [shards(): hess = lax.psum(high_dot(coefs, coefs.T), 'snap') + RIDGE * eye]
  transfers between devices with their start and end apart: 8 -> 14, of which waited for: 4 -> 6; matrix products, arithmetic and copies ran while one was open for 12% -> 18% of each run, Pallas kernels for 0% -> 0%
where the time goes in v1:
time: 720 us; the launch traced here: 715 us
  blocking collectives  271 us (38%)
  waiting for transfers between devices  202 us (28%)
  matrix products  103 us (14%)
  other arithmetic  99.3 us (14%)
  between operations  18.9 us (3%)
  starting transfers between devices  12.8 us (2%)
    psum x6, blocking collectives, clipped_error(): total = lax.psum(jnp.sum(error * error), ('pts', 'snap'))  242 us
    psum x2, waiting for transfers between devices, shards(): hess = lax.psum(high_dot(coefs, coefs.T), 'snap') + RIDGE * eye  137 us
    dot_general x16, matrix products, high_dot(): jnp.dot(left, right, preferred_element_type=jnp.float32, precision=lax.Pr...  94.2 us
    reduce_scatter x4, waiting for transfers between devices, shards(): share = lax.psum_scatter(product, 'pts', scatter_dimension=1, tiled=True)  44 us
    all_gather x4, blocking collectives, shards(): coefs = lax.all_gather(own, 'pts', axis=1, tiled=True)  29.3 us
    another operation x6, other arithmetic, shards(): factor = jnp.linalg.cholesky(gram)  24.8 us
    another operation x6, other arithmetic, shards(): hfactor = jnp.linalg.cholesky(hess)  24.8 us
    ppermute x6, waiting for transfers between devices, shards(): lax.ppermute(summed, 'snap', [(i, i ^ far) for i in range(count_2)])  21.2 us
  transfers between devices with their start and end apart: 14, of which 6 were waited for; matrix products, arithmetic and copies ran while one was open for 18% of the time, Pallas kernels for 0%

profile of v1, /device:TPU:0, one launch (start us, length us, event | category | flops | bytes accessed | tf_op | source)
XLA Modules:
  0.0 714.8 jit_solution(13857297258475927996)
XLA Ops:
  10.1 8.6 %multiply_reduce_fusion.5 = (f32[]{:T(128)}, f32[1024,1024]{1,0:T(8,128)}) fusion(f32[1024,1024]{1,0:T(8,128)} %param.8, f32[1024,128]{1,0:T(8,128)} %param.9, f32[128,1024]{1,0:T(8,128)} %param.10), kind=kOutput, calls=%fused_computation.25 | convolution fusion | flops 1613758464 | bytes 9437188 | tf_op jit(solution)/shard_map/dot_general | solution.py:13
  18.8 42.5 %psum.71 = f32[]{:T(128)} all-reduce(f32[]{:T(128)} %get-tuple-element.7), channel_id=1, replica_groups=mesh['pts'=4,'snap'=8] {'pts','snap'}, use_global_device_ids=true, to_apply=%region_4.6 | all-reduce | flops 1 | bytes 8 | tf_op jit(solution)/shard_map/psum | solution.py:18
  61.9 9.6 %fusion.32 = f32[128,1024]{0,1:T(8,128)} fusion(f32[1024,128]{1,0:T(8,128)S(1)} %copy-done, f32[1024,1024]{1,0:T(8,128)} %get-tuple-element.8, f32[]{:T(128)S(6)} %neg.18, f32[]{:T(128)S(6)} %mul.63), kind=kOutput, calls=%fused_computation.46 | convolution fusion | flops 1612709888 | bytes 5242888 | tf_op jit(solution)/shard_map/dot_general | solution.py:13
  79.4 11.7 %cholesky.74 = f32[128,128]{1,0:T(8,128)S(1)} custom-call(f32[128,128]{1,0:T(8,128)S(1)} %fusion.67), custom_call_target="Cholesky" | custom-call | tf_op jit(solution)/shard_map/jit(cholesky)/cholesky | solution.py:33
  92.4 9.8 %custom-call.16 = f32[1,128,128]{1,2,0:T(8,128)S(1)} custom-call(f32[1,128,128]{2,1,0:T(8,128)S(1)} %fusion.44), custom_call_target="InvertDiagBlocksLowerTriangular" | custom-call | tf_op jit(solution)/shard_map/jit(_cho_solve)/triangular_solve | solution.py:40
  104.7 8.0 %all_gather.12 = f32[128,1024]{1,0:T(8,128)S(1)} all-gather(f32[128,256]{1,0:T(8,128)S(1)} %convolution_add_fusion.3), channel_id=1, replica_groups=mesh['pts'=4,'snap'=8] {'pts'}, dimensions={1}, use_global_device_ids=true | all-gather | bytes 655360 | tf_op jit(solution)/shard_map/all_gather | solution.py:41
  112.6 7.7 %multiply_reduce_fusion.4 = (f32[]{:T(128)}, f32[1024,1024]{0,1:T(8,128)}) fusion(f32[1024,1024]{0,1:T(8,128)} %copy.7, f32[128,1024]{1,0:T(8,128)S(1)} %all_gather.12, f32[1024,128]{1,0:T(8,128)S(1)} %copy-done), kind=kOutput, calls=%fused_computation.21 | convolution fusion | flops 1613758464 | bytes 9437188 | tf_op jit(solution)/shard_map/dot_general | solution.py:13
  120.3 39.7 %psum.72 = f32[]{:T(128)} all-reduce(f32[]{:T(128)} %get-tuple-element.9), channel_id=1, replica_groups=mesh['pts'=4,'snap'=8] {'pts','snap'}, use_global_device_ids=true, to_apply=%region_7.10 | all-reduce | flops 1 | bytes 8 | tf_op jit(solution)/shard_map/psum | solution.py:18
  167.2 22.0 %reduce-scatter.7.cloned.1.call-done = f32[128,256]{0,1:T(8,128)} async-done(((f32[128,1024]{0,1:T(8,128)}), f32[128,256]{0,1:T(8,128)}) %reduce-scatter.7.cloned.1.call-update) | async-done | bytes 131088 | tf_op jit(solution)/shard_map/reduce_scatter | solution.py:37
  190.7 6.6 all_gather.13
  197.3 7.6 %multiply_reduce_fusion.3 = (f32[]{:T(128)}, f32[1024,1024]{0,1:T(8,128)}) fusion(f32[1024,1024]{0,1:T(8,128)} %copy.7, f32[128,1024]{1,0:T(8,128)S(1)} %all_gather.13, f32[1024,128]{1,0:T(8,128)S(1)} %copy-done), kind=kOutput, calls=%fused_computation.17 | convolution fusion | flops 1613758464 | bytes 9437188 | tf_op jit(solution)/shard_map/dot_general | solution.py:13
  204.9 40.0 %psum.74 = f32[]{:T(128)} all-reduce(f32[]{:T(128)} %get-tuple-element.11), channel_id=1, replica_groups=mesh['pts'=4,'snap'=8] {'pts','snap'}, use_global_device_ids=true, to_apply=%region_11.14 | all-reduce | flops 1 | bytes 8 | tf_op jit(solution)/shard_map/psum | solution.py:18
  245.6 8.5 %fusion.9 = f32[1024,128]{1,0:T(8,128)S(1)} fusion(f32[128,1024]{1,0:T(8,128)S(1)} %all_gather.13, f32[1024,1024]{0,1:T(8,128)} %get-tuple-element.12, f32[]{:T(128)S(6)} %neg.20, f32[]{:T(128)S(6)} %mul.67), kind=kOutput, calls=%fused_computation.14 | convolution fusion | flops 1612709888 | bytes 5242888 | tf_op jit(solution)/shard_map/dot_general | solution.py:13
  256.6 10.6 %collective-permute-done = f32[1024,128]{1,0:T(8,128)S(1)} collective-permute-done((f32[1024,128]{1,0:T(8,128)S(1)}, f32[1024,128]{1,0:T(8,128)S(1)}, u32[]{:S(2)}, u32[]{:S(2)}) %collective-permute-start) | collective-permute-done | bytes 524320 | tf_op jit(solution)/shard_map/ppermute | solution.py:49
  270.5 68.7 %all-reduce.7.cloned.1.call-done = f32[128,128]{0,1:T(8,128)} async-done(((f32[128,128]{0,1:T(8,128)}), f32[128,128]{0,1:T(8,128)}) %all-reduce.7.cloned.1.call-update) | async-done | bytes 65552 | tf_op jit(solution)/shard_map/psum | solution.py:43
  342.9 11.7 %cholesky.85 = f32[128,128]{1,0:T(8,128)S(1)} custom-call(f32[128,128]{1,0:T(8,128)S(1)} %fusion.60), custom_call_target="Cholesky" | custom-call | tf_op jit(solution)/shard_map/jit(cholesky)/cholesky | solution.py:44
  355.9 9.8 %custom-call.18 = f32[1,128,128]{1,2,0:T(8,128)S(1)} custom-call(f32[1,128,128]{2,1,0:T(8,128)S(1)} %fusion.45), custom_call_target="InvertDiagBlocksLowerTriangular" | custom-call | tf_op jit(solution)/shard_map/jit(_cho_solve)/triangular_solve | solution.py:51
  368.2 7.6 %multiply_reduce_fusion.2 = (f32[]{:T(128)}, f32[1024,1024]{1,0:T(8,128)}) fusion(f32[1024,1024]{1,0:T(8,128)} %param.8, f32[1024,128]{0,1:T(8,128)S(1)} %fusion.30, f32[128,1024]{1,0:T(8,128)S(1)} %all_gather.13), kind=kOutput, calls=%fused_computation.13 | convolution fusion | flops 1613758464 | bytes 9437188 | tf_op jit(solution)/shard_map/dot_general | solution.py:13
  375.8 40.4 %psum.76 = f32[]{:T(128)} all-reduce(f32[]{:T(128)} %get-tuple-element.13), channel_id=1, replica_groups=mesh['pts'=4,'snap'=8] {'pts','snap'}, use_global_device_ids=true, to_apply=%region_14.18 | all-reduce | flops 1 | bytes 8 | tf_op jit(solution)/shard_map/psum | solution.py:18
  424.6 11.7 %cholesky.96 = f32[128,128]{1,0:T(8,128)S(1)} custom-call(f32[128,128]{1,0:T(8,128)S(1)} %fusion.57), custom_call_target="Cholesky" | custom-call | tf_op jit(solution)/shard_map/jit(cholesky)/cholesky | solution.py:33
  437.6 9.8 %custom-call.19 = f32[1,128,128]{1,2,0:T(8,128)S(1)} custom-call(f32[1,128,128]{2,1,0:T(8,128)S(1)} %fusion.46), custom_call_target="InvertDiagBlocksLowerTriangular" | custom-call | tf_op jit(solution)/shard_map/jit(_cho_solve)/triangular_solve | solution.py:40
  448.9 8.1 %all_gather.14 = f32[128,1024]{1,0:T(8,128)S(1)} all-gather(f32[128,256]{1,0:T(8,128)S(1)} %convolution_add_fusion.1), channel_id=1, replica_groups=mesh['pts'=4,'snap'=8] {'pts'}, dimensions={1}, use_global_device_ids=true | all-gather | bytes 655360 | tf_op jit(solution)/shard_map/all_gather | solution.py:41
  457.1 7.6 %multiply_reduce_fusion.1 = (f32[]{:T(128)}, f32[1024,1024]{1,0:T(8,128)}) fusion(f32[1024,1024]{1,0:T(8,128)} %param.8, f32[1024,128]{0,1:T(8,128)S(1)} %fusion.30, f32[128,1024]{1,0:T(8,128)S(1)} %all_gather.14), kind=kOutput, calls=%fused_computation.9 | convolution fusion | flops 1613758464 | bytes 9437188 | tf_op jit(solution)/shard_map/dot_general | solution.py:13
  464.7 38.9 %psum.77 = f32[]{:T(128)} all-reduce(f32[]{:T(128)} %get-tuple-element.15), channel_id=1, replica_groups=mesh['pts'=4,'snap'=8] {'pts','snap'}, use_global_device_ids=true, to_apply=%region_17.21 | all-reduce | flops 1 | bytes 8 | tf_op jit(solution)/shard_map/psum | solution.py:18
  510.0 22.0 %reduce-scatter.11.cloned.1.call-done = f32[128,256]{1,0:T(8,128)} async-done(((f32[128,1024]{1,0:T(8,128)}), f32[128,256]{1,0:T(8,128)}) %reduce-scatter.11.cloned.1.call-update) | async-done | bytes 131088 | tf_op jit(solution)/shard_map/reduce_scatter | solution.py:37
  533.5 6.6 all_gather.15
  540.1 7.6 %multiply_reduce_fusion = (f32[]{:T(128)}, f32[1024,1024]{1,0:T(8,128)}) fusion(f32[1024,1024]{1,0:T(8,128)} %param.8, f32[1024,128]{0,1:T(8,128)S(1)} %fusion.30, f32[128,1024]{1,0:T(8,128)S(1)} %all_gather.15), kind=kOutput, calls=%fused_computation.5 | convolution fusion | flops 1613758464 | bytes 9437188 | tf_op jit(solution)/shard_map/dot_general | solution.py:13
  547.6 40.2 %psum.79 = f32[]{:T(128)} all-reduce(f32[]{:T(128)} %get-tuple-element.17), channel_id=1, replica_groups=mesh['pts'=4,'snap'=8] {'pts','snap'}, use_global_device_ids=true, to_apply=%region_21.25 | all-reduce | flops 1 | bytes 8 | tf_op jit(solution)/shard_map/psum | solution.py:18
  596.4 10.6 %collective-permute-done.3 = f32[1024,128]{1,0:T(8,128)S(1)} collective-permute-done((f32[1024,128]{1,0:T(8,128)S(1)}, f32[1024,128]{1,0:T(8,128)S(1)}, u32[]{:S(2)}, u32[]{:S(2)}) %collective-permute-start.3) | collective-permute-done | bytes 524320 | tf_op jit(solution)/shard_map/ppermute | solution.py:49
  610.6 68.3 %all-reduce.11.cloned.1.call-done = f32[128,128]{0,1:T(8,128)} async-done(((f32[128,128]{0,1:T(8,128)}), f32[128,128]{0,1:T(8,128)}) %all-reduce.11.cloned.1.call-update) | async-done | bytes 65552 | tf_op jit(solution)/shard_map/psum | solution.py:43
  682.6 11.7 %cholesky.107 = f32[128,128]{1,0:T(8,128)S(1)} custom-call(f32[128,128]{1,0:T(8,128)S(1)} %fusion.50), custom_call_target="Cholesky" | custom-call | tf_op jit(solution)/shard_map/jit(cholesky)/cholesky | solution.py:44
  695.7 9.8 %custom-call.21 = f32[1,128,128]{1,2,0:T(8,128)S(1)} custom-call(f32[1,128,128]{2,1,0:T(8,128)S(1)} %fusion.47), custom_call_target="InvertDiagBlocksLowerTriangular" | custom-call | tf_op jit(solution)/shard_map/jit(_cho_solve)/triangular_solve | solution.py:51
  (84 shorter events, 71.9 us)
Async XLA Ops:
  7.2 70.4 %all-reduce.5.cloned.1.call-start = ((), (), s32[]{:S(2)}) async-start(), calls=%async_computation.4 | async-start | bytes 131072 | tf_op jit(solution)/shard_map/psum | solution.py:32
  10.1 51.8 %copy-start = (f32[1024,128]{1,0:T(8,128)S(1)}, f32[1024,128]{1,0:T(8,128)}, u32[]{:S(2)}) copy-start(f32[1024,128]{1,0:T(8,128)} %param.9) | copy-start | bytes 1572868
  10.1 92.2 %reduce-scatter.5.cloned.1.call-start = ((), (), s32[]{:S(2)}) async-start(), calls=%async_computation.5 | async-start | bytes 655360 | tf_op jit(solution)/shard_map/reduce_scatter | solution.py:37
  71.6 117.6 %reduce-scatter.7.cloned.1.call-start = ((), (), s32[]{:S(2)}) async-start(), calls=%async_computation.6 | async-start | bytes 655360 | tf_op jit(solution)/shard_map/reduce_scatter | solution.py:37
  167.1 172.1 %all-reduce.7.cloned.1.call-start = ((), (), s32[]{:S(2)}) async-start(), calls=%async_computation.7 | async-start | bytes 131072 | tf_op jit(solution)/shard_map/psum | solution.py:43
  254.1 13.1 %collective-permute-start = (f32[1024,128]{1,0:T(8,128)S(1)}, f32[1024,128]{1,0:T(8,128)S(1)}, u32[]{:S(2)}, u32[]{:S(2)}) collective-permute-start(f32[1024,128]{1,0:T(8,128)S(1)} %fusion.9), channel_id=1, source_target_pairs={{0,1},{1,0},{2,3},{3,2},{4,5},{5,4},{6,7},{7,6},{8,9},{9,8},{10,11... | collective-permute-start | bytes 1572872 | tf_op jit(solution)/shard_map/ppermute | solution.py:49
  267.3 72.9 %collective-permute-start.1 = (f32[1024,128]{1,0:T(8,128)S(1)}, f32[1024,128]{1,0:T(8,128)S(1)}, u32[]{:S(2)}, u32[]{:S(2)}) collective-permute-start(f32[1024,128]{1,0:T(8,128)S(1)} %add.123), channel_id=1, source_target_pairs={{0,2},{1,3},{2,0},{3,1},{4,6},{5,7},{6,4},{7,5},{8,10},{9,11},{10,... | collective-permute-start | bytes 1572872 | tf_op jit(solution)/shard_map/ppermute | solution.py:49
  270.1 152.7 %all-reduce.9.cloned.1.call-start = ((), (), s32[]{:S(2)}) async-start(), calls=%async_computation.8 | async-start | bytes 131072 | tf_op jit(solution)/shard_map/psum | solution.py:32
  340.2 25.5 %collective-permute-start.2 = (f32[1024,128]{1,0:T(8,128)S(1)}, f32[1024,128]{1,0:T(8,128)S(1)}, u32[]{:S(2)}, u32[]{:S(2)}) collective-permute-start(f32[1024,128]{1,0:T(8,128)S(1)} %add.124), channel_id=1, source_target_pairs={{0,4},{1,5},{2,6},{3,7},{4,0},{5,1},{6,2},{7,3},{8,12},{9,13},{10,... | collective-permute-start | bytes 1572872 | tf_op jit(solution)/shard_map/ppermute | solution.py:49
  375.8 71.7 %reduce-scatter.9.cloned.1.call-start = ((), (), s32[]{:S(2)}) async-start(), calls=%async_computation.9 | async-start | bytes 655360 | tf_op jit(solution)/shard_map/reduce_scatter | solution.py:37
  422.7 109.3 %reduce-scatter.11.cloned.1.call-start = ((), (), s32[]{:S(2)}) async-start(), calls=%async_computation.10 | async-start | bytes 655360 | tf_op jit(solution)/shard_map/reduce_scatter | solution.py:37
  510.0 169.0 %all-reduce.11.cloned.1.call-start = ((), (), s32[]{:S(2)}) async-start(), calls=%async_computation.11 | async-start | bytes 131072 | tf_op jit(solution)/shard_map/psum | solution.py:43
  593.8 13.1 %collective-permute-start.3 = (f32[1024,128]{1,0:T(8,128)S(1)}, f32[1024,128]{1,0:T(8,128)S(1)}, u32[]{:S(2)}, u32[]{:S(2)}) collective-permute-start(f32[1024,128]{1,0:T(8,128)S(1)} %fusion), channel_id=1, source_target_pairs={{0,1},{1,0},{2,3},{3,2},{4,5},{5,4},{6,7},{7,6},{8,9},{9,8},{10,11... | collective-permute-start | bytes 1572872 | tf_op jit(solution)/shard_map/ppermute | solution.py:49
  607.0 72.9 %collective-permute-start.4 = (f32[1024,128]{1,0:T(8,128)S(1)}, f32[1024,128]{1,0:T(8,128)S(1)}, u32[]{:S(2)}, u32[]{:S(2)}) collective-permute-start(f32[1024,128]{1,0:T(8,128)S(1)} %add.134), channel_id=1, source_target_pairs={{0,2},{1,3},{2,0},{3,1},{4,6},{5,7},{6,4},{7,5},{8,10},{9,11},{10,... | collective-permute-start | bytes 1572872 | tf_op jit(solution)/shard_map/ppermute | solution.py:49
  680.0 25.5 %collective-permute-start.5 = (f32[1024,128]{1,0:T(8,128)S(1)}, f32[1024,128]{1,0:T(8,128)S(1)}, u32[]{:S(2)}, u32[]{:S(2)}) collective-permute-start(f32[1024,128]{1,0:T(8,128)S(1)} %add.135), channel_id=1, source_target_pairs={{0,4},{1,5},{2,6},{3,7},{4,0},{5,1},{6,2},{7,3},{8,12},{9,13},{10,... | collective-permute-start | bytes 1572872 | tf_op jit(solution)/shard_map/ppermute | solution.py:49
Sparse Core Ops, SparseCore 0:
  10.9 34.2 all-reduce.4
  71.7 21.8 reduce-scatter.4
  167.2 21.8 reduce-scatter.6
  270.2 68.9 all-reduce.6
  375.9 31.3 all-reduce.8
  422.8 21.1 reduce-scatter.8
  510.1 21.8 reduce-scatter.10
  609.9 68.9 all-reduce.10
